TPU v7x, 128 devices: a whole 4x4x4 slice. The times are simulated.
128 devices in a mesh: section: 8 (over y, core), fsdp: 16 (over x, z).
Axes of the slice: x: 4, y: 4, z: 4, core: 2. Of those that a mesh axis runs over, the one named last changes fastest.
Arguments:
- layer_input: bfloat16 [8, 8192, 2048], P('section', 'fsdp'), may hold values from -6 to 6
- resid_grad: bfloat16 [8, 8192, 2048], P('section', 'fsdp'), may hold values from -6 to 6
- qkv_grad: bfloat16 [8, 8192, 3072], P('section', 'fsdp'), may hold values from -6 to 6
- prev_input: bfloat16 [8, 8192, 2048], P('section', 'fsdp'), may hold values from -6 to 6
- prev_qkv_grad: bfloat16 [8, 8192, 3072], P('section', 'fsdp'), may hold values from -0.059814453 to 0.059814453
- qkv_weight: bfloat16 [8, 2048, 3072], P('section', 'fsdp'), may hold values from -0.125 to 0.125
- norm_gain: float32 [8, 2048], P('section'), may hold values from 0.1 to 1.9
Outputs:
- upstream_grad: bfloat16 [8, 8192, 2048], P('section', 'fsdp')
- weight_grad: float32 [8, 2048, 3072], P('section', 'fsdp')
- gain_grad: float32 [8, 2048], P('section')
All inputs are finite; a program needn't handle non-finite values.
Results may differ from a plain program's by a relative error of at most 0.018.
Values may be sent and summed in bfloat16 or wider, within the bound.
A program may use at most 128 MiB of HBM per device.

v0:
```python
import jax
import jax.numpy as jnp
from jax import lax
from jax.sharding import PartitionSpec as P

EPS = 1e-05


def from_behind(block, axis, distance):
    devices = range(lax.axis_size(axis))
    route = [(i - distance, i) for i in devices if i - distance in devices]
    return lax.ppermute(block, axis, route)


def row_scale(rows):
    values = rows.astype(jnp.float32)
    return lax.rsqrt(jnp.mean(values * values, axis=-1, keepdims=True) + EPS)


def transpose_product(grads, piece):
    return lax.dot_general(
        grads, piece, (((1,), (1,)), ((), ())), preferred_element_type=jnp.float32
    )


def local(layer_input, resid_grad, qkv_grad, prev_input, prev_qkv_grad, qkv_weight, norm_gain):
    rows_now = layer_input[0]
    grads_now = qkv_grad[0]
    rows_prev = prev_input[0]
    grads_prev = prev_qkv_grad[0]
    weight_rows = qkv_weight[0]
    gain = norm_gain[0]
    owned = weight_rows.shape[0]
    prev_scale = row_scale(rows_prev)
    prev_normed = (rows_prev.astype(jnp.float32) * prev_scale * gain[None, :]).astype(jnp.bfloat16)
    direction = transpose_product(
        grads_now, lax.all_gather(weight_rows, "fsdp", axis=0, tiled=True)
    )
    scale = row_scale(rows_now)
    values = rows_now.astype(jnp.float32)
    gained = gain[None, :] * direction
    inner = jnp.mean(gained * values, axis=-1, keepdims=True)
    local_grad = (
        resid_grad[0].astype(jnp.float32) + scale * gained - values * scale * scale * scale * inner
    ).astype(jnp.bfloat16)
    upstream_grad = from_behind(local_grad, "section", -1)
    upstream_grad, ready_rows = lax.optimization_barrier((upstream_grad, prev_normed))
    weight_grad = lax.psum_scatter(
        lax.dot_general(
            ready_rows, grads_prev, (((0,), (0,)), ((), ())), preferred_element_type=jnp.float32
        ).astype(jnp.bfloat16),
        "fsdp",
        scatter_dimension=0,
        tiled=True,
    ).astype(jnp.float32)
    owned_gain = lax.dynamic_slice_in_dim(gain, lax.axis_index("fsdp") * owned, owned, 0)
    gain_part = jnp.sum(weight_rows.astype(jnp.float32) * weight_grad, axis=1) / owned_gain
    gain_grad = lax.all_gather(gain_part, "fsdp", axis=0, tiled=True)
    return (upstream_grad[None], weight_grad[None], gain_grad[None])


def solution(mesh):
    placed = (
        P("section", "fsdp", None),
        P("section", "fsdp", None),
        P("section", "fsdp", None),
        P("section", "fsdp", None),
        P("section", "fsdp", None),
        P("section", "fsdp", None),
        P("section", None),
    )
    return jax.shard_map(
        local,
        mesh=mesh,
        in_specs=placed,
        out_specs=(P("section", "fsdp", None), P("section", "fsdp", None), P("section", None)),
        check_vma=False,
    )
```

profile of v0, /device:TPU:0, one launch (start us, length us, event | category | flops | bytes accessed | tf_op | source)
XLA Modules:
  0.0 288.5 jit_solution(17675918492956940125)
XLA Ops:
  7.2 0.0 copy-start
  7.2 0.0 all-gather.4.cloned.1.call-start
  7.2 0.7 all-gather.4.cloned.1.call-update
  7.9 0.0 reduce-scatter.2.cloned.1.call-start
  8.0 2.2 fusion.2
  10.2 92.6 %all-gather.4.cloned.1.call-done = bf16[1,2048,3072]{2,1,0:T(8,128)(2,1)} async-done(((bf16[1,128,3072]{2,1,0:T(8,128)(2,1)}), bf16[1,2048,3072]{2,1,0:T(8,128)(2,1)}) %all-gather.4.cloned.1.call-update) | async-done | bytes 12582928 | tf_op jit(solution)/shard_map/all_gather | solution.py:37
  102.8 0.0 copy-start.1
  102.8 15.5 %fusion.5 = (f32[512]{0:T(512)S(1)}, f32[512]{0:T(512)S(1)}, bf16[512,2048]{1,0:T(8,128)(2,1)}, f32[512,2048]{1,0:T(8,128)}) fusion(bf16[1,512,2048]{2,1,0:T(8,128)(2,1)} %param.7, f32[2048]{0:T(1024)} %bitcast.41, f32[512]{0:T(512)S(1)} %add_rsqrt_fusion, bf16[1,512,2048]{2,1,0:T(8,128)(2,1)} %param.10, ...), kind=kOutput, calls=%fused_computation.11 | convolution fusion | flops 6452935680 | bytes 26228736 | tf_op jit(solution)/shard_map/dot_general | solution.py:21
  118.3 0.0 copy-done.1
  118.3 0.0 copy-start.2
  118.4 5.3 %fusion.10 = bf16[512,2048]{1,0:T(8,128)(2,1)S(1)} fusion(f32[512,2048]{1,0:T(8,128)} %get-tuple-element.10, bf16[1,512,2048]{2,1,0:T(8,128)(2,1)} %param.8, bf16[1,512,2048]{2,1,0:T(8,128)(2,1)} %param.7, f32[512]{0:T(512)S(1)} %get-tuple-element.12, f32[2048]{0:T(1024)S(1)} %bitcast.42, f32[512]{0:T(512)S(1)} %get-tuple-element.11), kind=kLoop, calls=%fused_computation.16 | loop fusion | flops 11534336 | bytes 10498048 | tf_op jit(solution)/shard_map/convert_element_type | solution.py:45
  123.6 1.3 collective-permute-start
  124.9 4.9 %collective-permute-done = bf16[512,2048]{1,0:T(8,128)(2,1)} collective-permute-done((bf16[512,2048]{1,0:T(8,128)(2,1)S(1)}, bf16[512,2048]{1,0:T(8,128)(2,1)}, u32[]{:S(2)}, u32[]{:S(2)}) %collective-permute-start) | collective-permute-done | bytes 2097184 | tf_op jit(solution)/shard_map/ppermute | solution.py:12
  129.8 0.0 copy-done
  129.8 0.0 copy-done.2
  129.8 9.7 %convolution_convert_fusion = bf16[2048,3072]{1,0:T(8,128)(2,1)} fusion(bf16[512,2048]{1,0:T(8,128)(2,1)S(1)} %copy-done.2, bf16[1,512,3072]{2,1,0:T(8,128)(2,1)S(1)} %copy-done), kind=kOutput, calls=%fused_computation.2 | convolution fusion | flops 6448742400 | bytes 17825792 | tf_op jit(solution)/shard_map/dot_general | solution.py:49
  139.5 0.0 reduce-scatter.2.cloned.1.call-update
  139.6 114.9 %reduce-scatter.2.cloned.1.call-done = bf16[128,3072]{1,0:T(8,128)(2,1)} async-done(((bf16[2048,3072]{1,0:T(8,128)(2,1)}), bf16[128,3072]{1,0:T(8,128)(2,1)}) %reduce-scatter.2.cloned.1.call-update) | async-done | bytes 786448 | tf_op jit(solution)/shard_map/reduce_scatter | solution.py:48
  254.4 1.7 fusion.14
  256.1 19.3 %all-gather.1 = f32[16,1,128]{2,1,0:T(1,128)S(1)} all-gather(f32[1,1,128]{2,1,0:T(1,128)S(1)} %fusion.15), channel_id=1, replica_groups=mesh['section'=8,'fsdp'=16] {'fsdp'}, dimensions={0}, use_global_device_ids=true | all-gather | bytes 8704 | tf_op jit(solution)/shard_map/all_gather | solution.py:58
  275.4 2.4 convert_bitcast_fusion
  277.9 3.2 %copy.12 = bf16[1,512,2048]{2,1,0:T(8,128)(2,1)} copy(bf16[1,512,2048]{2,1,0:T(8,128)(2,1)} %bitcast.8) | data formatting | bytes 4194304
  281.0 0.6 copy.13
  (3 shorter events, 0.0 us)
Async XLA Ops:
  7.2 122.7 %copy-start = (bf16[1,512,3072]{2,1,0:T(8,128)(2,1)S(1)}, bf16[1,512,3072]{2,1,0:T(8,128)(2,1)}, u32[]{:S(2)}) copy-start(bf16[1,512,3072]{2,1,0:T(8,128)(2,1)} %param.11) | copy-start | bytes 9437188
  7.2 95.7 %all-gather.4.cloned.1.call-start = ((), (), s32[]{:S(2)}) async-start(), calls=%async_computation.2 | async-start | bytes 13369344 | tf_op jit(solution)/shard_map/all_gather | solution.py:37
  7.9 246.5 %reduce-scatter.2.cloned.1.call-start = ((), (), s32[]{:S(2)}) async-start(), calls=%async_computation.1 | async-start | bytes 13369344 | tf_op jit(solution)/shard_map/reduce_scatter | solution.py:48
  102.8 15.5 %copy-start.1 = (f32[1,2048]{1,0:T(1,128)S(1)}, f32[1,2048]{1,0:T(1,128)}, u32[]{:S(2)}) copy-start(f32[1,2048]{1,0:T(1,128)} %param.13) | copy-start | bytes 24580
  118.3 11.5 %copy-start.2 = (bf16[512,2048]{1,0:T(8,128)(2,1)S(1)}, bf16[512,2048]{1,0:T(8,128)(2,1)}, u32[]{:S(2)}) copy-start(bf16[512,2048]{1,0:T(8,128)(2,1)} %get-tuple-element.6) | copy-start | bytes 6291460
  123.6 6.2 %collective-permute-start = (bf16[512,2048]{1,0:T(8,128)(2,1)S(1)}, bf16[512,2048]{1,0:T(8,128)(2,1)}, u32[]{:S(2)}, u32[]{:S(2)}) collective-permute-start(bf16[512,2048]{1,0:T(8,128)(2,1)S(1)} %fusion.10), channel_id=1, source_target_pairs={{16,0},{32,16},{48,32},{64,48},{80,64},{96,80},{112,96},{17,1},{33... | collective-permute-start | bytes 6291464 | tf_op jit(solution)/shard_map/ppermute | solution.py:12
Sparse Core Ops, SparseCore 0:
  10.2 92.5 all-gather.3
  139.7 114.6 reduce-scatter.1
where the time goes:
time: 289 us; the launch traced here: 288 us
  waiting for transfers between devices  213 us (74%)
  matrix products  25.2 us (9%)
  blocking collectives  19.3 us (7%)
  between operations  14.1 us (5%)
  other arithmetic  11.6 us (4%)
  local copies, waits for them, and re-layouts  3.78 us (1%)
    reduce_scatter x1, waiting for transfers between devices, local(): lax.psum_scatter(lax.dot_general(ready_rows, grads_prev, (((0,), (0,)), (...  115 us
    all_gather x1, waiting for transfers between devices, local(): lax.all_gather(weight_rows, 'fsdp', axis=0, tiled=True)  92.6 us
    all_gather x1, blocking collectives, local(): gain_grad = lax.all_gather(gain_part, 'fsdp', axis=0, tiled=True)  19.3 us
    dot_general x1, matrix products, transpose_product(): lax.dot_general(grads, piece, (((1,), (1,)), ((), ())), preferred_element...  15.5 us
    dot_general x1, matrix products, local(): lax.dot_general(ready_rows, grads_prev, (((0,), (0,)), ((), ())), preferr...  9.72 us
  transfers between devices with their start and end apart: 3, of which 3 were waited for; matrix products, arithmetic and copies ran while one was open for 1% of the time, Pallas kernels for 0%

commit v1 on v0

--- a/solution.py
+++ b/solution.py
@@ -55,7 +55,8 @@
     ).astype(jnp.float32)
     owned_gain = lax.dynamic_slice_in_dim(gain, lax.axis_index("fsdp") * owned, owned, 0)
     gain_part = jnp.sum(weight_rows.astype(jnp.float32) * weight_grad, axis=1) / owned_gain
-    gain_grad = lax.all_gather(gain_part, "fsdp", axis=0, tiled=True)
+    sent = jnp.stack([gain_part] * lax.axis_size("fsdp"))
+    gain_grad = jnp.concatenate(lax.all_to_all(sent, "fsdp", 0, 0), axis=0)
     return (upstream_grad[None], weight_grad[None], gain_grad[None])
 
 

time: 289 us -> 280 us (0.969)
  blocking collectives: 19.3 us -> 0 us
  waiting for transfers between devices: 213 us -> 218 us
  starting transfers between devices: 1.37 us -> 5.98 us
    all_gather x1 -> x0, blocking collectives: 19.3 us -> none  [local(): gain_grad = lax.all_gather(gain_part, 'fsdp', axis=0, tiled=True)]
    all_to_all x0 -> x1, waiting for transfers between devices: none -> 5.05 us  [local(): gain_grad = jnp.concatenate(lax.all_to_all(sent, 'fsdp', 0, 0), axis=0)]
    all_to_all x0 -> x1, starting transfers between devices: none -> 4.62 us  [local(): gain_grad = jnp.concatenate(lax.all_to_all(sent, 'fsdp', 0, 0), axis=0)]
  transfers between devices with their start and end apart: 3 -> 4, of which waited for: 3 -> 4; matrix products, arithmetic and copies ran while one was open for 1% -> 2% of each run, Pallas kernels for 0% -> 0%
where the time goes in v1:
time: 280 us; the launch traced here: 279 us
  waiting for transfers between devices  218 us (78%)
  matrix products  25.2 us (9%)
  between operations  14.1 us (5%)
  other arithmetic  11.6 us (4%)
  starting transfers between devices  5.98 us (2%)
  local copies, waits for them, and re-layouts  4.38 us (2%)
    reduce_scatter x1, waiting for transfers between devices, local(): lax.psum_scatter(lax.dot_general(ready_rows, grads_prev, (((0,), (0,)), (...  115 us
    all_gather x1, waiting for transfers between devices, local(): lax.all_gather(weight_rows, 'fsdp', axis=0, tiled=True)  92.6 us
    dot_general x1, matrix products, transpose_product(): lax.dot_general(grads, piece, (((1,), (1,)), ((), ())), preferred_element...  15.5 us
    dot_general x1, matrix products, local(): lax.dot_general(ready_rows, grads_prev, (((0,), (0,)), ((), ())), preferr...  9.72 us
  transfers between devices with their start and end apart: 4, of which 4 were waited for; matrix products, arithmetic and copies ran while one was open for 2% of the time, Pallas kernels for 0%

profile of v1, /device:TPU:0, one launch (start us, length us, event | category | flops | bytes accessed | tf_op | source)
XLA Modules:
  0.0 279.4 jit_solution(3791839593174945489)
XLA Ops:
  7.2 0.0 copy-start
  7.2 0.0 all-gather.3.cloned.1.call-start
  7.2 0.7 all-gather.3.cloned.1.call-update
  7.9 0.0 reduce-scatter.2.cloned.1.call-start
  8.0 2.2 fusion.2
  10.2 92.6 %all-gather.3.cloned.1.call-done = bf16[1,2048,3072]{2,1,0:T(8,128)(2,1)} async-done(((bf16[1,128,3072]{2,1,0:T(8,128)(2,1)}), bf16[1,2048,3072]{2,1,0:T(8,128)(2,1)}) %all-gather.3.cloned.1.call-update) | async-done | bytes 12582928 | tf_op jit(solution)/shard_map/all_gather | solution.py:37
  102.8 15.5 %fusion.5 = (f32[512]{0:T(512)S(1)}, f32[512]{0:T(512)S(1)}, bf16[512,2048]{1,0:T(8,128)(2,1)}, f32[512,2048]{1,0:T(8,128)}) fusion(bf16[1,512,2048]{2,1,0:T(8,128)(2,1)} %param.7, f32[2048]{0:T(1024)} %bitcast.41, f32[512]{0:T(512)S(1)} %add_rsqrt_fusion, bf16[1,512,2048]{2,1,0:T(8,128)(2,1)} %param.10, ...), kind=kOutput, calls=%fused_computation.11 | convolution fusion | flops 6452935680 | bytes 26228736 | tf_op jit(solution)/shard_map/dot_general | solution.py:21
  118.3 0.0 copy-done.1
  118.3 0.0 copy-start.2
  118.4 5.3 %fusion.10 = bf16[512,2048]{1,0:T(8,128)(2,1)S(1)} fusion(f32[512,2048]{1,0:T(8,128)} %get-tuple-element.10, bf16[1,512,2048]{2,1,0:T(8,128)(2,1)} %param.8, bf16[1,512,2048]{2,1,0:T(8,128)(2,1)} %param.7, f32[512]{0:T(512)S(1)} %get-tuple-element.12, f32[2048]{0:T(1024)S(1)} %bitcast.42, f32[512]{0:T(512)S(1)} %get-tuple-element.11), kind=kLoop, calls=%fused_computation.16 | loop fusion | flops 11534336 | bytes 10498048 | tf_op jit(solution)/shard_map/convert_element_type | solution.py:45
  123.6 1.3 collective-permute-start
  124.9 4.9 %collective-permute-done = bf16[512,2048]{1,0:T(8,128)(2,1)} collective-permute-done((bf16[512,2048]{1,0:T(8,128)(2,1)S(1)}, bf16[512,2048]{1,0:T(8,128)(2,1)}, u32[]{:S(2)}, u32[]{:S(2)}) %collective-permute-start) | collective-permute-done | bytes 2097184 | tf_op jit(solution)/shard_map/ppermute | solution.py:12
  129.8 0.0 copy-done
  129.8 0.0 copy-done.2
  129.8 9.7 %convolution_convert_fusion = bf16[2048,3072]{1,0:T(8,128)(2,1)} fusion(bf16[512,2048]{1,0:T(8,128)(2,1)S(1)} %copy-done.2, bf16[1,512,3072]{2,1,0:T(8,128)(2,1)S(1)} %copy-done), kind=kOutput, calls=%fused_computation.2 | convolution fusion | flops 6448742400 | bytes 17825792 | tf_op jit(solution)/shard_map/dot_general | solution.py:49
  139.5 0.0 reduce-scatter.2.cloned.1.call-update
  139.6 114.9 %reduce-scatter.2.cloned.1.call-done = bf16[128,3072]{1,0:T(8,128)(2,1)} async-done(((bf16[2048,3072]{1,0:T(8,128)(2,1)}), bf16[128,3072]{1,0:T(8,128)(2,1)}) %reduce-scatter.2.cloned.1.call-update) | async-done | bytes 786448 | tf_op jit(solution)/shard_map/reduce_scatter | solution.py:48
  254.4 1.7 fusion.14
  256.1 0.6 stack.2
  256.7 4.6 %all-to-all-start = ((f32[16,1,128]{2,1,0:T(1,128)}), f32[16,1,128]{2,1,0:T(1,128)S(1)}, u32[]{:S(2)}, u32[]{:S(2)}) async-start(f32[16,1,128]{2,1,0:T(1,128)} %stack.2), calls=%async_computation.1 | async-start | bytes 16384 | tf_op jit(solution)/shard_map/all_to_all | solution.py:59
  261.3 2.4 convert_bitcast_fusion
  263.8 5.1 %all-to-all-done = f32[16,1,128]{2,1,0:T(1,128)S(1)} async-done(((f32[16,1,128]{2,1,0:T(1,128)}), f32[16,1,128]{2,1,0:T(1,128)S(1)}, u32[]{:S(2)}, u32[]{:S(2)}) %all-to-all-start) | async-done | bytes 8224 | tf_op jit(solution)/shard_map/all_to_all | solution.py:59
  268.8 3.2 %copy.12 = bf16[1,512,2048]{2,1,0:T(8,128)(2,1)} copy(bf16[1,512,2048]{2,1,0:T(8,128)(2,1)} %bitcast.8) | data formatting | bytes 4194304
  272.0 0.6 copy.13
  (4 shorter events, 0.0 us)
Async XLA Ops:
  7.2 122.7 %copy-start = (bf16[1,512,3072]{2,1,0:T(8,128)(2,1)S(1)}, bf16[1,512,3072]{2,1,0:T(8,128)(2,1)}, u32[]{:S(2)}) copy-start(bf16[1,512,3072]{2,1,0:T(8,128)(2,1)} %param.11) | copy-start | bytes 9437188
  7.2 95.7 %all-gather.3.cloned.1.call-start = ((), (), s32[]{:S(2)}) async-start(), calls=%async_computation.3 | async-start | bytes 13369344 | tf_op jit(solution)/shard_map/all_gather | solution.py:37
  7.9 246.5 %reduce-scatter.2.cloned.1.call-start = ((), (), s32[]{:S(2)}) async-start(), calls=%async_computation.2 | async-start | bytes 13369344 | tf_op jit(solution)/shard_map/reduce_scatter | solution.py:48
  102.8 15.5 %copy-start.1 = (f32[1,2048]{1,0:T(1,128)S(1)}, f32[1,2048]{1,0:T(1,128)}, u32[]{:S(2)}) copy-start(f32[1,2048]{1,0:T(1,128)} %param.13) | copy-start | bytes 24580
  118.3 11.5 %copy-start.2 = (bf16[512,2048]{1,0:T(8,128)(2,1)S(1)}, bf16[512,2048]{1,0:T(8,128)(2,1)}, u32[]{:S(2)}) copy-start(bf16[512,2048]{1,0:T(8,128)(2,1)} %get-tuple-element.6) | copy-start | bytes 6291460
  123.6 6.2 %collective-permute-start = (bf16[512,2048]{1,0:T(8,128)(2,1)S(1)}, bf16[512,2048]{1,0:T(8,128)(2,1)}, u32[]{:S(2)}, u32[]{:S(2)}) collective-permute-start(bf16[512,2048]{1,0:T(8,128)(2,1)S(1)} %fusion.10), channel_id=1, source_target_pairs={{16,0},{32,16},{48,32},{64,48},{80,64},{96,80},{112,96},{17,1},{33... | collective-permute-start | bytes 6291464 | tf_op jit(solution)/shard_map/ppermute | solution.py:12
  256.7 12.1 %all-to-all-start = ((f32[16,1,128]{2,1,0:T(1,128)}), f32[16,1,128]{2,1,0:T(1,128)S(1)}, u32[]{:S(2)}, u32[]{:S(2)}) async-start(f32[16,1,128]{2,1,0:T(1,128)} %stack.2), calls=%async_computation.1 | async-start | bytes 16384 | tf_op jit(solution)/shard_map/all_to_all | solution.py:59
Sparse Core Ops, SparseCore 0:
  10.2 92.5 all-gather.2
  139.7 114.6 reduce-scatter.1
